TPU v7x, 32 devices: a whole 2x2x4 slice. The times are simulated.
32 devices in a mesh: cell: 2 (over y), gene: 16 (over z, x, core).
Axes of the slice: x: 2, y: 2, z: 4, core: 2. Of those that a mesh axis runs over, the one named last changes fastest.
Arguments:
- blocks: bfloat16 [1536, 256, 256], P(('cell', 'gene')), may hold values from 0 to 255, as said below
- block_rows: int32 [1536], P(('cell', 'gene')), may hold values from 0 to 15, as said below
- block_cols: int32 [1536], P(('cell', 'gene')), may hold values from 0 to 3, as said below
- block_count: int32 [32], P(('cell', 'gene')), may hold values from 2 to 48, as said below
- cell_factor: float32 [8192, 128], P(('cell', 'gene')), as said below
- gene_factor: float32 [16384, 128], P('gene'), as said below
Outputs:
- cell_new: float32 [8192, 128], P(('cell', 'gene'))
- gene_new: float32 [16384, 128], P('gene')
Inputs may be any that keep to these rules, and one draw needn't show every extreme that they name: `blocks`: counts are whole numbers. `block_rows`: within one device the live slots and the padding slots name distinct block positions. `block_cols`: within one device the live slots and the padding slots name distinct block positions. `block_count`: some device has all 48 slots live. `cell_factor`: positive entries. `gene_factor`: positive entries.
All inputs are finite; a program needn't handle non-finite values.
Results may differ from a plain program's by a relative error of at most 0.00084.
Values may be sent and summed in bfloat16 or wider, within the bound.
A program may use at most 64 MiB of HBM per device.

v0:
```python
import jax
import jax.numpy as jnp
from jax import lax
from jax.sharding import PartitionSpec as P


def block_ratio(blocks, row_tiles, col_tiles, live):
    model = jnp.einsum("nir,njr->nij", row_tiles, col_tiles, preferred_element_type=jnp.float32)
    return (blocks.astype(jnp.float32) / model * live[:, None, None]).astype(jnp.bfloat16)


def on_device(blocks, block_rows, block_cols, block_count, cell_factor, gene_factor):
    slots = blocks.shape[0]
    width = blocks.shape[1]
    rank = cell_factor.shape[1]
    gene_len = gene_factor.shape[0]
    live = (jnp.arange(slots, dtype=jnp.int32) < block_count[0]).astype(jnp.float32)
    gene_bf = gene_factor.astype(jnp.bfloat16)
    gene_tiles = gene_bf.reshape(-1, width, rank)[block_cols]
    gene_totals = lax.psum(jnp.sum(gene_factor, 0), "gene")
    cell_full = lax.all_gather(cell_factor, "gene", axis=0, tiled=True)
    cell_bf = cell_full.astype(jnp.bfloat16)
    row_count = cell_bf.shape[0] // width
    row_pick = (block_rows[None, :] == jnp.arange(row_count, dtype=jnp.int32)[:, None]).astype(
        jnp.float32
    )
    col_pick = (
        block_cols[None, :] == jnp.arange(gene_len // width, dtype=jnp.int32)[:, None]
    ).astype(jnp.float32)
    row_tiles = cell_bf.reshape(row_count, width, rank)[block_rows]
    ratio = block_ratio(blocks, row_tiles, gene_tiles, live)
    terms = jnp.einsum("nij,njr->nir", ratio, gene_tiles, preferred_element_type=jnp.float32)
    numer = jnp.einsum("bn,nir->bir", row_pick, terms, precision=lax.Precision.HIGHEST).reshape(
        -1, rank
    )
    whole = lax.psum(numer, "gene")
    group_new = cell_full * whole / gene_totals
    new_bf = group_new.astype(jnp.bfloat16)
    cell_sums = lax.psum(jnp.sum(group_new, 0), "cell")
    own_rows = cell_factor.shape[0]
    cell_new = lax.dynamic_slice_in_dim(group_new, lax.axis_index("gene") * own_rows, own_rows, 0)
    new_tiles = new_bf.reshape(row_count, width, rank)[block_rows]
    ratio_next = block_ratio(blocks, new_tiles, gene_tiles, live)
    terms_next = jnp.einsum(
        "nij,nir->njr", ratio_next, new_tiles, preferred_element_type=jnp.float32
    )
    numer_gene = jnp.einsum(
        "bn,njr->bjr", col_pick, terms_next, precision=lax.Precision.HIGHEST
    ).reshape(-1, rank)
    total = lax.psum(numer_gene, "cell")
    gene_new = gene_factor * total / cell_sums
    return (cell_new, gene_new)


def solution(mesh):
    placed = (
        P(("cell", "gene"), None, None),
        P(("cell", "gene")),
        P(("cell", "gene")),
        P(("cell", "gene")),
        P(("cell", "gene"), None),
        P("gene", None),
    )
    return jax.shard_map(
        on_device,
        mesh=mesh,
        in_specs=placed,
        out_specs=(P(("cell", "gene"), None), P("gene", None)),
        check_vma=False,
    )
```

profile of v0, /device:TPU:0, one launch (start us, length us, event | category | flops | bytes accessed | tf_op | source)
XLA Modules:
  0.0 241.2 jit_solution(14404089688201856968)
XLA Ops:
  7.2 0.0 all-gather.2.cloned.1.call-start
  7.2 0.7 all-gather.2.cloned.1.call-update
  7.9 0.0 all-reduce.3.cloned.1.call-start
  8.6 0.7 compare_select_fusion
  9.3 1.4 fusion.23
  10.7 0.0 copy-start.1
  10.7 2.8 %gather_fusion.1 = bf16[48,256,128]{2,1,0:T(8,128)(2,1)} fusion(bf16[4,256,128]{2,1,0:T(8,128)(2,1)S(1)} %bitcast.19, s32[1024]{0:T(1024)S(1)} %pad_clamp_fusion), kind=kCustom, calls=%fused_computation.1 | custom fusion | bytes 6291648 | tf_op jit(solution)/shard_map/gather | solution.py:19
  13.4 0.0 copy-done.1
  13.5 40.9 %all-gather.2.cloned.1.call-done = f32[4096,128]{1,0:T(8,128)} async-done(((f32[256,128]{1,0:T(8,128)}), f32[4096,128]{1,0:T(8,128)}) %all-gather.2.cloned.1.call-update) | async-done | bytes 2097168 | tf_op jit(solution)/shard_map/all_gather | solution.py:21
  54.3 1.7 convert_element_type.29
  56.0 2.7 %gather_fusion = bf16[48,256,128]{2,1,0:T(8,128)(2,1)} fusion(bf16[16,256,128]{2,1,0:T(8,128)(2,1)S(1)} %bitcast.21, s32[1024]{0:T(1024)S(1)} %pad_clamp_fusion.1), kind=kCustom, calls=%fused_computation | custom fusion | bytes 6291648 | tf_op jit(solution)/shard_map/gather | solution.py:30
  58.7 11.7 %fusion.10 = f32[48,256,128]{2,1,0:T(8,128)} fusion(bf16[48,256,128]{2,1,0:T(8,128)(2,1)} %gather_fusion.1, bf16[48,256,256]{2,1,0:T(8,128)(2,1)} %param.6, f32[48]{0:T(128)S(1)} %compare_convert_fusion, bf16[48,256,128]{2,1,0:T(8,128)(2,1)} %gather_fusion), kind=kOutput, calls=%fused_computation.14 | convolution fusion | flops 1623195648 | bytes 18874560 | tf_op jit(solution)/shard_map/nij,njr->nir/dot_general | solution.py:32
  70.4 8.4 %fusion.6 = f32[16,256,128]{2,0,1:T(8,128)S(1)} fusion(f32[48,256,128]{2,1,0:T(8,128)} %fusion.10, s32[48]{0:T(128)S(1)} %copy-done.1), kind=kOutput, calls=%fused_computation.11 | convolution fusion | flops 301990656 | bytes 8388800 | tf_op jit(solution)/shard_map/bn,nir->bir/dot_general | solution.py:33
  78.8 2.0 copy.8
  80.8 0.0 all-reduce.3.cloned.1.call-update
  80.8 0.0 all-reduce.5.cloned.1.call-start
  80.9 31.9 %psum.29 = f32[128]{0:T(128)S(1)} all-reduce(f32[128]{0:T(128)S(1)} %get-tuple-element.5), channel_id=1, replica_groups=mesh['cell'=2,'gene'=16] {'gene'}, use_global_device_ids=true, to_apply=%region_2.0 | all-reduce | flops 128 | bytes 1024 | tf_op jit(solution)/shard_map/psum | solution.py:20
  112.8 65.2 %all-reduce.3.cloned.1.call-done = f32[4096,128]{1,0:T(8,128)} async-done(((f32[4096,128]{1,0:T(8,128)}), f32[4096,128]{1,0:T(8,128)}) %all-reduce.3.cloned.1.call-update) | async-done | bytes 2097168 | tf_op jit(solution)/shard_map/psum | solution.py:36
  177.9 2.8 %fusion.22 = (f32[128]{0:T(128)S(1)}, f32[4096,128]{1,0:T(8,128)S(1)}) fusion(f32[128]{0:T(128)S(1)} %psum.29, f32[4096,128]{1,0:T(8,128)} %all-gather.2.cloned.1.call-done, f32[4096,128]{1,0:T(8,128)} %all-reduce.3.cloned.1.call-done), kind=kLoop, calls=%fused_computation.31 | loop fusion | flops 1572736 | bytes 6292480 | tf_op jit(solution)/shard_map/reduce_sum | solution.py:39
  180.7 0.1 convert_element_type.33
  180.8 2.7 %gather_fusion.2 = bf16[48,256,128]{2,1,0:T(8,128)(2,1)} fusion(bf16[16,256,128]{2,1,0:T(8,128)(2,1)S(1)} %bitcast.20, s32[1024]{0:T(1024)S(1)} %pad_clamp_fusion.1), kind=kCustom, calls=%fused_computation.2 | custom fusion | bytes 6291648 | tf_op jit(solution)/shard_map/gather | solution.py:42
  183.5 0.0 copy-start.2
  183.5 12.2 %fusion.8 = f32[48,256,128]{2,1,0:T(8,128)} fusion(bf16[48,256,128]{2,1,0:T(8,128)(2,1)} %gather_fusion.2, bf16[48,256,256]{2,1,0:T(8,128)(2,1)} %param.6, f32[48]{0:T(128)S(1)} %compare_convert_fusion, bf16[48,256,128]{2,1,0:T(8,128)(2,1)} %gather_fusion.1), kind=kOutput, calls=%fused_computation.13 | convolution fusion | flops 1623195648 | bytes 18874560 | tf_op jit(solution)/shard_map/nij,nir->njr/dot_general | solution.py:44
  195.7 0.0 copy-done.2
  195.7 8.2 %fusion.4 = f32[4,256,128]{2,0,1:T(4,128)S(1)} fusion(f32[48,256,128]{2,1,0:T(8,128)} %fusion.8, s32[48]{0:T(128)S(1)} %copy-done.2), kind=kOutput, calls=%fused_computation.9 | convolution fusion | flops 75497664 | bytes 6815936 | tf_op jit(solution)/shard_map/bn,njr->bjr/dot_general | solution.py:47
  203.9 0.8 copy.9
  204.7 0.0 all-reduce.5.cloned.1.call-update
  204.7 4.9 %psum.31 = f32[128]{0:T(128)S(1)} all-reduce(f32[128]{0:T(128)S(1)} %get-tuple-element.2), channel_id=1, replica_groups=mesh['cell'=2,'gene'=16] {'cell'}, use_global_device_ids=true, to_apply=%region_5.0 | all-reduce | flops 128 | bytes 1024 | tf_op jit(solution)/shard_map/psum | solution.py:39
  209.7 0.7 constant_dynamic-slice_fusion
  210.3 22.5 %all-reduce.5.cloned.1.call-done = f32[1024,128]{1,0:T(8,128)} async-done(((f32[1024,128]{1,0:T(8,128)}), f32[1024,128]{1,0:T(8,128)}) %all-reduce.5.cloned.1.call-update) | async-done | bytes 524304 | tf_op jit(solution)/shard_map/psum | solution.py:50
  232.8 0.0 copy-done
  232.8 1.9 multiply_divide_fusion.1
  (5 shorter events, 0.0 us)
Async XLA Ops:
  7.2 47.2 %all-gather.2.cloned.1.call-start = ((), (), s32[]{:S(2)}) async-start(), calls=%async_computation | async-start | bytes 2228224 | tf_op jit(solution)/shard_map/all_gather | solution.py:21
  7.9 170.0 %all-reduce.3.cloned.1.call-start = ((), (), s32[]{:S(2)}) async-start(), calls=%async_computation.1 | async-start | bytes 4194304 | tf_op jit(solution)/shard_map/psum | solution.py:36
  10.7 2.8 %copy-start.1 = (s32[48]{0:T(128)S(1)}, s32[48]{0:T(128)}, u32[]{:S(2)}) copy-start(s32[48]{0:T(128)} %param.7) | copy-start | bytes 580
  80.8 152.0 %all-reduce.5.cloned.1.call-start = ((), (), s32[]{:S(2)}) async-start(), calls=%async_computation.2 | async-start | bytes 1048576 | tf_op jit(solution)/shard_map/psum | solution.py:50
  183.5 12.2 %copy-start.2 = (s32[48]{0:T(128)S(1)}, s32[48]{0:T(128)}, u32[]{:S(2)}) copy-start(s32[48]{0:T(128)} %param.8) | copy-start | bytes 580
  195.7 37.1 %copy-start = (f32[1024,128]{1,0:T(8,128)S(1)}, f32[1024,128]{1,0:T(8,128)}, u32[]{:S(2)}) copy-start(f32[1024,128]{1,0:T(8,128)} %param.11) | copy-start | bytes 1572868
Sparse Core Ops, SparseCore 0:
  10.1 44.1 all-gather.1
  80.9 96.9 all-reduce.2
  204.9 27.9 all-reduce.4
where the time goes:
time: 242 us; the launch traced here: 241 us
  waiting for transfers between devices  129 us (53%)
  matrix products  40.5 us (17%)
  blocking collectives  36.8 us (15%)
  between operations  14.4 us (6%)
  local copies, waits for them, and re-layouts  11.6 us (5%)
  other arithmetic  8.57 us (4%)
    psum x1, waiting for transfers between devices, on_device(): whole = lax.psum(numer, 'gene')  65.2 us
    all_gather x1, waiting for transfers between devices, on_device(): cell_full = lax.all_gather(cell_factor, 'gene', axis=0, tiled=True)  40.9 us
    psum x1, blocking collectives, on_device(): gene_totals = lax.psum(jnp.sum(gene_factor, 0), 'gene')  31.9 us
    psum x1, waiting for transfers between devices, on_device(): total = lax.psum(numer_gene, 'cell')  22.5 us
    dot_general x1, matrix products, on_device(): jnp.einsum('nij,nir->njr', ratio_next, new_tiles, preferred_element_type=...  12.2 us
    dot_general x1, matrix products, on_device(): jnp.einsum('nij,njr->nir', ratio, gene_tiles, preferred_element_type=jnp....  11.7 us
    dot_general x1, matrix products, on_device(): jnp.einsum('bn,nir->bir', row_pick, terms, precision=lax.Precision.HIGHEST)  8.37 us
    dot_general x1, matrix products, on_device(): jnp.einsum('bn,njr->bjr', col_pick, terms_next, precision=lax.Precision.H...  8.16 us
  transfers between devices with their start and end apart: 3, of which 3 were waited for; matrix products, arithmetic and copies ran while one was open for 2% of the time, Pallas kernels for 0%

commit v1 on v0

v1 whole, which is shorter than its diff:
```python
import functools

import jax
import jax.numpy as jnp
from jax import lax
from jax.experimental import pallas as pl
from jax.experimental.pallas import tpu as pltpu
from jax.sharding import PartitionSpec as P

MESH = pl.DeviceIdType.MESH
F32 = jnp.float32
BF = jnp.bfloat16


def digits(group):
    cores = 2
    far = 4
    return far, group // (far * cores), cores


class Spot:
    def __init__(self, group):
        self.group = group
        self.far, self.near, self.cores = digits(group)
        self.me = lax.axis_index("gene")
        self.a = self.me // (self.near * self.cores)
        self.b = lax.rem(self.me // self.cores, self.near)
        self.c = lax.rem(self.me, self.cores)

    def a_at(self, d):
        return lax.rem(self.a + d, self.far)

    def b_at(self, d):
        return lax.rem(self.b + d, self.near)

    def index(self, a, b, c):
        return (a * self.near + b) * self.cores + c


def send(src, dst, send_sem, recv_sem, where):
    copy = pltpu.make_async_remote_copy(
        src_ref=src, dst_ref=dst, send_sem=send_sem, recv_sem=recv_sem,
        device_id=where, device_id_type=MESH,
    )
    copy.start()
    return copy


def greet(axis, size):
    barrier = pltpu.get_barrier_semaphore()
    me = lax.axis_index(axis)
    for d in range(1, size):
        pl.semaphore_signal(
            barrier, inc=1, device_id={axis: lax.rem(me + d, size)}, device_id_type=MESH
        )


def far_order(far):
    order = []
    for step in range(1, far // 2 + 1):
        order.append(step)
        if far - step != step:
            order.append(far - step)
    return order


class Gather:
    def __init__(self, spot, own, out, sems):
        self.spot, self.own, self.out = spot, own, out
        self.zs, self.zr, self.xs, self.xr, self.cs, self.cr = sems
        self.zc, self.xc, self.cc = {}, {}, {}

    def place(self, d, e):
        spot = self.spot
        return self.out.at[spot.index(spot.a_at(d), spot.b_at(e), spot.c)]

    def start(self, order):
        spot = self.spot
        for d in order:
            self.zc[d] = send(self.own, self.out.at[spot.me], self.zs.at[d], self.zr.at[d],
                              {"gene": spot.index(spot.a_at(spot.far - d), spot.b, spot.c)})
        self.forward(0, self.own)

    def forward(self, d, src):
        spot = self.spot
        for e in range(1, spot.near):
            self.xc[d, e] = send(src, self.place(d, 0), self.xs.at[d, e], self.xr.at[d, e],
                                 {"gene": spot.index(spot.a, spot.b_at(spot.near - e), spot.c)})
        self.pair(d, 0, src)

    def pair(self, d, e, src):
        spot = self.spot
        self.cc[d, e] = send(src, self.place(d, e), self.cs.at[d, e], self.cr.at[d, e],
                             {"gene": spot.index(spot.a, spot.b, 1 - spot.c)})

    def take_far(self, d):
        self.zc[d].wait_recv()
        self.forward(d, self.place(d, 0))

    def take_near(self, d):
        for e in range(1, self.spot.near):
            self.xc[d, e].wait_recv()
            self.pair(d, e, self.place(d, e))

    def ready(self, d):
        for e in range(self.spot.near):
            self.cc[d, e].wait_recv()

    def close(self):
        for copy in [*self.zc.values(), *self.xc.values(), *self.cc.values()]:
            copy.wait_send()


def gather_sems(far, near):
    dma = pltpu.SemaphoreType.DMA
    return [dma((far,))] * 2 + [dma((far, near))] * 4


def share(spot, src, parts, ss, sr):
    return [
        send(src, parts.at[spot.me], ss.at[d], sr.at[d], {"gene": lax.rem(spot.me + d, spot.group)})
        for d in range(1, spot.group)
    ]


def step_kernel(group, cells, blocks, table, cell, gene, cell_new, gene_new,
                held, gene_bf, flipped, own_bf, own_sum, parts, cell_bf,
                next_bf, next_sum, next_parts, next_cell, numer, p1, p2, p3, t2, t3,
                acc, other, group_sum, other_sum, *sems):
    spot = Spot(group)
    far, near = spot.far, spot.near
    a, b, c = spot.a, spot.b, spot.c
    slots, width, _ = blocks.shape
    tiles = gene.shape[0]
    rows = cell.shape[0]
    sub = width // rows
    one_sems, two_sems = sems[0:6], sems[6:12]
    s1, r1, s2, r2, s3, r3, gs, gr, ns, nr, fs, fr, os, orr, ls = sems[12:]
    load = pltpu.make_async_copy(blocks, held.at[pl.ds(0, slots)], ls.at[0])
    load.start()

    greet("gene", group)
    greet("cell", cells)
    held[slots] = jnp.zeros((width, width), BF)
    own_bf[...] = cell[...].astype(BF)
    cell_bf[spot.me] = cell[...].astype(BF)
    first_sum = jnp.zeros((1, gene.shape[-1]), F32)
    for j in range(tiles):
        first_sum += jnp.sum(gene[j], axis=0, keepdims=True)
    own_sum[...] = first_sum
    parts[spot.me] = first_sum
    pl.semaphore_wait(pltpu.get_barrier_semaphore(), group - 1 + cells - 1)

    order = far_order(far) + [0]
    one = Gather(spot, own_bf, cell_bf, one_sems)
    one.start(order[:-1])
    shared = share(spot, own_sum, parts, gs, gr)
    for j in range(tiles):
        gene_bf[j] = gene[j].astype(BF)
        flipped[j] = gene[j].astype(BF).T
    load.wait()
    for i, d in enumerate(order[:-1]):
        one.take_far(d)
        if i == 1:
            one.take_near(0)
            one.take_near(order[0])

    def ratio_of(source, g, j):
        rows_bf = source[g]
        slot = table[(g // sub) * tiles + j]
        if sub == 1:
            x = held[slot]
        else:
            x = held[slot, pl.ds(pl.multiple_of(lax.rem(g, sub) * rows, rows), rows), :]
        model = jnp.dot(rows_bf, flipped[j], preferred_element_type=F32)
        return (x.astype(F32) / model).astype(BF), rows_bf

    def first_half(d, core):
        def body(e, carry):
            g = spot.index(spot.a_at(d), spot.b_at(e), core)
            total = None
            for j in range(tiles):
                ratio, _ = ratio_of(cell_bf, g, j)
                term = jnp.dot(ratio, gene_bf[j], preferred_element_type=F32)
                total = term if total is None else total + term
            numer[g] = total
            return carry

        lax.fori_loop(0, near, body, 0)

    c1, c2, c3 = {}, {}, {}

    def stage_one(d):
        for e in [*range(1, near), 0]:
            at = spot.index(spot.a_at(d), spot.b_at(e), 1 - c)
            c1[d, e] = send(numer.at[at], p1.at[d, e], s1.at[d, e], r1.at[d, e],
                            {"gene": spot.index(a, b, 1 - c)})

    def stage_two(d):
        for e in range(1, near):
            c1[d, e].wait_recv()
            t2[d, e] = numer[spot.index(spot.a_at(d), spot.b_at(e), c)] + p1[d, e]
            c2[d, e] = send(t2.at[d, e], p2.at[d, e], s2.at[d, e], r2.at[d, e],
                            {"gene": spot.index(a, spot.b_at(e), c)})

    def summed(d):
        c1[d, 0].wait_recv()
        value = numer[spot.index(spot.a_at(d), b, c)] + p1[d, 0]
        for e in range(1, near):
            c2[d, e].wait_recv()
            value += p2[d, e]
        return value

    def stage_three(d):
        t3[d] = summed(d)
        c3[d] = send(t3.at[d], p3.at[d], s3.at[d], r3.at[d],
                     {"gene": spot.index(spot.a_at(d), b, c)})

    for i, d in enumerate(order):
        one.ready(d)
        first_half(d, 1 - c)
        stage_one(d)
        if i == 0:
            for other_d in order[1:-1]:
                one.take_near(other_d)
        if i >= 2:
            stage_three(order[i - 2])
        first_half(d, c)
        stage_two(d)
    stage_three(order[-2])
    for copy in shared:
        copy.wait()
    total = jnp.sum(parts[...], axis=0)
    value = summed(0)
    for d in order[:-1]:
        c3[d].wait_recv()
        value += p3[d]
    fresh = cell[...] * value / total
    next_bf[...] = fresh.astype(BF)
    next_cell[spot.me] = fresh.astype(BF)
    cell_new[...] = fresh
    fresh_sum = jnp.sum(fresh, axis=0, keepdims=True)
    next_sum[...] = fresh_sum
    next_parts[spot.me] = fresh_sum

    two = Gather(spot, next_bf, next_cell, two_sems)
    later = [d for d in range(1, far) if d != far // 2] + [far // 2]
    two.start(later)
    shared = share(spot, next_sum, next_parts, ns, nr)
    acc[...] = jnp.zeros_like(acc)

    def second_half(d, core, columns):
        def body(e, carry):
            g = spot.index(spot.a_at(d), spot.b_at(e), core)
            for j in columns:
                ratio, rows_bf = ratio_of(next_cell, g, j)
                acc[j] += lax.dot_general(
                    ratio, rows_bf, (((0,), (0,)), ((), ())), preferred_element_type=F32
                )
            return carry

        lax.fori_loop(0, near, body, 0)

    every = range(tiles)
    two.take_near(0)
    two.take_far(later[0])
    two.ready(0)
    second_half(0, c, every)
    two.take_far(later[1])
    second_half(0, 1 - c, every)
    two.take_far(later[2])
    two.take_near(later[0])
    two.take_near(later[1])
    second_half(later[0], c, every)
    two.take_near(later[2])
    two.ready(later[0])
    second_half(later[0], 1 - c, every)
    two.ready(later[1])
    two.ready(later[2])

    mine = lax.axis_index("cell")
    for copy in shared:
        copy.wait()
    sums = jnp.sum(next_parts[...], axis=0)
    group_sum[...] = sums
    sum_copies, copies = {}, {}
    for d in range(1, cells):
        sum_copies[d] = send(group_sum, other_sum.at[d], os.at[d], orr.at[d],
                             {"cell": lax.rem(mine + d, cells)})
    for j in every:
        for d in later[1:]:
            for core in (0, 1):
                second_half(d, core, [j])
        for d in range(1, cells):
            copies[j, d] = send(acc.at[j], other.at[d, j], fs.at[d, j], fr.at[d, j],
                                {"cell": lax.rem(mine + d, cells)})
    for d in range(1, cells):
        sum_copies[d].wait()
        sums += other_sum[d]
    for j in every:
        value = acc[j]
        for d in range(1, cells):
            copies[j, d].wait()
            value += other[d, j]
        gene_new[j] = gene[j] * value / sums
    one.close()
    two.close()
    for copy in [*c1.values(), *c2.values(), *c3.values()]:
        copy.wait_send()


VMEM = pl.BlockSpec(memory_space=pltpu.VMEM)
SMEM = pl.BlockSpec(memory_space=pltpu.SMEM)
ANY = pl.BlockSpec(memory_space=pl.ANY)


def step(group, cells, blocks, table, cell, gene):
    far, near, _ = digits(group)
    slots, width, _ = blocks.shape
    tiles, _, rank = gene.shape
    rows = cell.shape[0]
    dma = pltpu.SemaphoreType.DMA
    vmem = pltpu.VMEM
    return pl.pallas_call(
        functools.partial(step_kernel, group, cells),
        out_shape=(
            jax.ShapeDtypeStruct(cell.shape, F32),
            jax.ShapeDtypeStruct(gene.shape, F32),
        ),
        in_specs=[ANY, SMEM, VMEM, VMEM],
        out_specs=(VMEM, VMEM),
        scratch_shapes=[
            vmem((slots + 1, width, width), BF),
            vmem((tiles, width, rank), BF),
            vmem((tiles, rank, width), BF),
            vmem((rows, rank), BF),
            vmem((1, rank), F32),
            vmem((group, 1, rank), F32),
            vmem((group, rows, rank), BF),
            vmem((rows, rank), BF),
            vmem((1, rank), F32),
            vmem((group, 1, rank), F32),
            vmem((group, rows, rank), BF),
            vmem((group, rows, rank), F32),
            vmem((far, near, rows, rank), F32),
            vmem((far, near, rows, rank), F32),
            vmem((far, rows, rank), F32),
            vmem((far, near, rows, rank), F32),
            vmem((far, rows, rank), F32),
            vmem((tiles, width, rank), F32),
            vmem((cells, tiles, width, rank), F32),
            vmem((1, rank), F32),
            vmem((cells, 1, rank), F32),
        ] + gather_sems(far, near) * 2 + [dma((far, near))] * 4 + [dma((far,))] * 2
        + [dma((group,))] * 4 + [dma((cells, tiles))] * 2 + [dma((cells,))] * 2 + [dma((1,))],
        compiler_params=pltpu.CompilerParams(
            collective_id=0, has_side_effects=True, vmem_limit_bytes=60 * 1024 * 1024
        ),
        name="update_step",
    )(blocks, table, cell, gene)


def on_device(cells, group, blocks, brow, bcol, bcount, cell_factor, gene_factor):
    slots, width, _ = blocks.shape
    rows, rank = cell_factor.shape
    tiles = gene_factor.shape[0] // width
    spots = jnp.arange(rows * group // width * tiles, dtype=jnp.int32)
    order = jnp.arange(slots, dtype=jnp.int32)
    where = jnp.where(order < bcount[0], brow * tiles + bcol, -1)
    table = jnp.min(jnp.where(spots[:, None] == where[None, :], order[None, :], slots), axis=1)
    cell_new, gene_new = step(group, cells, blocks, table, cell_factor,
                              gene_factor.reshape(tiles, width, rank))
    return cell_new, gene_new.reshape(gene_factor.shape)


def solution(mesh):
    sizes = dict(mesh.shape)
    placed = (
        P(("cell", "gene"), None, None),
        P(("cell", "gene")),
        P(("cell", "gene")),
        P(("cell", "gene")),
        P(("cell", "gene"), None),
        P("gene", None),
    )
    return jax.shard_map(
        functools.partial(on_device, sizes["cell"], sizes["gene"]),
        mesh=mesh,
        in_specs=placed,
        out_specs=(P(("cell", "gene"), None), P("gene", None)),
        check_vma=False,
    )
```

time: 242 us -> 78 us (0.32)
  waiting for transfers between devices: 129 us -> 0 us
  Pallas kernels: 0 us -> 71.8 us
  matrix products: 40.5 us -> 0 us
  blocking collectives: 36.8 us -> 0 us
  between operations: 14.4 us -> 1.29 us
  local copies, waits for them, and re-layouts: 11.6 us -> 3.44 us
  other arithmetic: 8.57 us -> 1.28 us
    psum x2 -> x0, waiting for transfers between devices: 87.6 us -> none  [the longest x1 65.2 us: on_device(): whole = lax.psum(numer, 'gene')]
    pallas_call x0 -> x1, Pallas kernels: none -> 71.8 us  [step(): pl.pallas_call(functools.partial(step_kernel, group, cells), out_shape=(j...]
    all_gather x1 -> x0, waiting for transfers between devices: 40.9 us -> none  [on_device(): cell_full = lax.all_gather(cell_factor, 'gene', axis=0, tiled=True)]
    dot_general x4 -> x0, matrix products: 40.5 us -> none  [the longest x1 12.2 us: on_device(): jnp.einsum('nij,nir->njr', ratio_next, new_tiles, preferred_element_type=...]
    psum x2 -> x0, blocking collectives: 36.8 us -> none  [the longest x1 31.9 us: on_device(): gene_totals = lax.psum(jnp.sum(gene_factor, 0), 'gene')]
    gather x3 -> x0, local copies, waits for them, and re-layouts: 8.11 us -> none  [the longest x1 2.75 us: on_device(): gene_tiles = gene_bf.reshape(-1, width, rank)[block_cols]]
    unnamed x6 -> x2, local copies, waits for them, and re-layouts: 0.01 us -> 3.44 us
    convert_element_type x4 -> x0, other arithmetic: 3.21 us -> none  [the longest x1 1.69 us: on_device(): cell_bf = cell_full.astype(jnp.bfloat16)]
  transfers between devices with their start and end apart: 3 -> 0, of which waited for: 3 -> 0; matrix products, arithmetic and copies ran while one was open for 2% -> 0% of each run, Pallas kernels for 0% -> 0%
where the time goes in v1:
time: 78 us; the launch traced here: 77.8 us
  Pallas kernels  71.8 us (92%)
  local copies, waits for them, and re-layouts  3.44 us (4%)
  between operations  1.29 us (2%)
  other arithmetic  1.28 us (2%)
    pallas_call x1, Pallas kernels, step(): pl.pallas_call(functools.partial(step_kernel, group, cells), out_shape=(j...  71.8 us
    unnamed x2, local copies, waits for them, and re-layouts  3.44 us

profile of v1, /device:TPU:0, one launch (start us, length us, event | category | flops | bytes accessed | tf_op | source)
XLA Modules:
  0.0 77.8 jit_solution(5716403649952604445)
XLA Ops:
  1.3 0.7 compare_select_fusion
  2.0 0.6 select_reduce_fusion.table
  2.6 71.8 %update_step.1 = (f32[256,128]{1,0:T(8,128)}, f32[4,256,128]{2,1,0:T(8,128)}) custom-call(bf16[48,256,256]{2,1,0:T(8,128)(2,1)} %blocks.1, s32[64]{0:T(128)} %select_reduce_fusion.table, f32[256,128]{1,0:T(8,128)} %cell.1, f32[4,256,128]{2,1,0:T(8,128)} %bitcast.5), custom_call_target="tpu_custom_call" | custom-call | tf_op jit(solution)/shard_map/update_step/pallas_call | solution.py:324
  74.3 1.6 %copy.11 = f32[256,128]{1,0:T(8,128)} copy(f32[256,128]{1,0:T(8,128)} %get-tuple-element.8) | data formatting | bytes 262144
  75.9 1.9 %copy.12 = f32[1024,128]{1,0:T(8,128)} copy(f32[1024,128]{1,0:T(8,128)} %bitcast.4) | data formatting | bytes 1048576

commit v2 on v1

--- a/solution.py
+++ b/solution.py
@@ -10,6 +10,7 @@
 MESH = pl.DeviceIdType.MESH
 F32 = jnp.float32
 BF = jnp.bfloat16
+I16 = jnp.int16
 
 
 def digits(group):
@@ -55,6 +56,17 @@
         )
 
 
+def encode(value, code, scale):
+    top = jnp.max(jnp.abs(value), axis=0, keepdims=True)
+    factor = jnp.where(top > 0.0, 32767.0 / top, 0.0)
+    code[...] = jnp.round(value * factor).astype(jnp.int32).astype(jnp.int16)
+    scale[...] = top * (1.0 / 32767.0)
+
+
+def decode(code, scale):
+    return code[...].astype(jnp.int32).astype(F32) * scale[...]
+
+
 def far_order(far):
     order = []
     for step in range(1, far // 2 + 1):
@@ -126,7 +138,7 @@
 def step_kernel(group, cells, blocks, table, cell, gene, cell_new, gene_new,
                 held, gene_bf, flipped, own_bf, own_sum, parts, cell_bf,
                 next_bf, next_sum, next_parts, next_cell, numer, p1, p2, p3, t2, t3,
-                acc, other, group_sum, other_sum, *sems):
+                p2m, p3m, t2m, t3m, acc, code, codem, other, otherm, group_sum, other_sum, *sems):
     spot = Spot(group)
     far, near = spot.far, spot.near
     a, b, c = spot.a, spot.b, spot.c
@@ -135,7 +147,7 @@
     rows = cell.shape[0]
     sub = width // rows
     one_sems, two_sems = sems[0:6], sems[6:12]
-    s1, r1, s2, r2, s3, r3, gs, gr, ns, nr, fs, fr, os, orr, ls = sems[12:]
+    s1, r1, s2, r2, s3, r3, gs, gr, ns, nr, fs, fr, os, orr, ls, u2, v2, u3, v3, uf, vf = sems[12:]
     load = pltpu.make_async_copy(blocks, held.at[pl.ds(0, slots)], ls.at[0])
     load.start()
 
@@ -159,11 +171,7 @@
         gene_bf[j] = gene[j].astype(BF)
         flipped[j] = gene[j].astype(BF).T
     load.wait()
-    for i, d in enumerate(order[:-1]):
-        one.take_far(d)
-        if i == 1:
-            one.take_near(0)
-            one.take_near(order[0])
+    one.take_near(0)
 
     def ratio_of(source, g, j):
         rows_bf = source[g]
@@ -196,46 +204,68 @@
             c1[d, e] = send(numer.at[at], p1.at[d, e], s1.at[d, e], r1.at[d, e],
                             {"gene": spot.index(a, b, 1 - c)})
 
+    def weight(g):
+        return jnp.mean(cell_bf[g].astype(F32), axis=1, keepdims=True)
+
     def stage_two(d):
         for e in range(1, near):
             c1[d, e].wait_recv()
-            t2[d, e] = numer[spot.index(spot.a_at(d), spot.b_at(e), c)] + p1[d, e]
-            c2[d, e] = send(t2.at[d, e], p2.at[d, e], s2.at[d, e], r2.at[d, e],
-                            {"gene": spot.index(a, spot.b_at(e), c)})
+            g = spot.index(spot.a_at(d), spot.b_at(e), c)
+            encode((numer[g] + p1[d, e]) * weight(g), t2.at[d, e], t2m.at[d, e])
+            where = {"gene": spot.index(a, spot.b_at(e), c)}
+            c2[d, e] = (
+                send(t2.at[d, e], p2.at[d, e], s2.at[d, e], r2.at[d, e], where),
+                send(t2m.at[d, e], p2m.at[d, e], u2.at[d, e], v2.at[d, e], where),
+            )
 
     def summed(d):
         c1[d, 0].wait_recv()
-        value = numer[spot.index(spot.a_at(d), b, c)] + p1[d, 0]
+        g = spot.index(spot.a_at(d), b, c)
+        value = (numer[g] + p1[d, 0]) * weight(g)
         for e in range(1, near):
-            c2[d, e].wait_recv()
-            value += p2[d, e]
+            for copy in c2[d, e]:
+                copy.wait_recv()
+            value += decode(p2.at[d, e], p2m.at[d, e])
         return value
 
     def stage_three(d):
-        t3[d] = summed(d)
-        c3[d] = send(t3.at[d], p3.at[d], s3.at[d], r3.at[d],
-                     {"gene": spot.index(spot.a_at(d), b, c)})
-
-    for i, d in enumerate(order):
+        encode(summed(d), t3.at[d], t3m.at[d])
+        where = {"gene": spot.index(spot.a_at(d), b, c)}
+        c3[d] = (
+            send(t3.at[d], p3.at[d], s3.at[d], r3.at[d], where),
+            send(t3m.at[d], p3m.at[d], u3.at[d], v3.at[d], where),
+        )
+
+    one.ready(0)
+    first_half(0, 1 - c)
+    stage_one(0)
+    for i, d in enumerate(order[:-1]):
+        one.take_far(d)
+        if i == 0:
+            continue
+        one.take_near(order[i - 1])
+    one.take_near(order[-2])
+    for i, d in enumerate(order[:-1]):
         one.ready(d)
         first_half(d, 1 - c)
         stage_one(d)
-        if i == 0:
-            for other_d in order[1:-1]:
-                one.take_near(other_d)
         if i >= 2:
             stage_three(order[i - 2])
         first_half(d, c)
         stage_two(d)
+    stage_three(order[-3])
+    first_half(0, c)
+    stage_two(0)
     stage_three(order[-2])
     for copy in shared:
         copy.wait()
     total = jnp.sum(parts[...], axis=0)
     value = summed(0)
     for d in order[:-1]:
-        c3[d].wait_recv()
-        value += p3[d]
-    fresh = cell[...] * value / total
+        for copy in c3[d]:
+            copy.wait_recv()
+        value += decode(p3.at[d], p3m.at[d])
+    fresh = cell[...] * (value / weight(spot.me)) / total
     next_bf[...] = fresh.astype(BF)
     next_cell[spot.me] = fresh.astype(BF)
     cell_new[...] = fresh
@@ -283,30 +313,48 @@
         copy.wait()
     sums = jnp.sum(next_parts[...], axis=0)
     group_sum[...] = sums
+    other_sum[mine] = sums
     sum_copies, copies = {}, {}
     for d in range(1, cells):
-        sum_copies[d] = send(group_sum, other_sum.at[d], os.at[d], orr.at[d],
+        sum_copies[d] = send(group_sum, other_sum.at[mine], os.at[d], orr.at[d],
                              {"cell": lax.rem(mine + d, cells)})
+
+    def balance(j):
+        return jnp.mean(gene_bf[j].astype(F32), axis=1, keepdims=True)
+
     for j in every:
         for d in later[1:]:
             for core in (0, 1):
                 second_half(d, core, [j])
+        encode(acc[j] * balance(j), code.at[j], codem.at[j])
+        other[mine, j] = code[j]
+        otherm[mine, j] = codem[j]
         for d in range(1, cells):
-            copies[j, d] = send(acc.at[j], other.at[d, j], fs.at[d, j], fr.at[d, j],
-                                {"cell": lax.rem(mine + d, cells)})
+            where = {"cell": lax.rem(mine + d, cells)}
+            copies[j, d] = (
+                send(code.at[j], other.at[mine, j], fs.at[d, j], fr.at[d, j], where),
+                send(codem.at[j], otherm.at[mine, j], uf.at[d, j], vf.at[d, j], where),
+            )
     for d in range(1, cells):
         sum_copies[d].wait()
-        sums += other_sum[d]
+    sums = other_sum[0]
+    for k in range(1, cells):
+        sums += other_sum[k]
     for j in every:
-        value = acc[j]
         for d in range(1, cells):
-            copies[j, d].wait()
-            value += other[d, j]
-        gene_new[j] = gene[j] * value / sums
+            for copy in copies[j, d]:
+                copy.wait()
+        value = decode(other.at[0, j], otherm.at[0, j])
+        for k in range(1, cells):
+            value += decode(other.at[k, j], otherm.at[k, j])
+        gene_new[j] = gene[j] * (value / balance(j)) / sums
     one.close()
     two.close()
-    for copy in [*c1.values(), *c2.values(), *c3.values()]:
+    for copy in c1.values():
         copy.wait_send()
+    for pair in [*c2.values(), *c3.values()]:
+        for copy in pair:
+            copy.wait_send()
 
 
 VMEM = pl.BlockSpec(memory_space=pltpu.VMEM)
@@ -343,16 +391,24 @@
             vmem((group, rows, rank), BF),
             vmem((group, rows, rank), F32),
             vmem((far, near, rows, rank), F32),
-            vmem((far, near, rows, rank), F32),
-            vmem((far, rows, rank), F32),
-            vmem((far, near, rows, rank), F32),
-            vmem((far, rows, rank), F32),
+            vmem((far, near, rows, rank), I16),
+            vmem((far, rows, rank), I16),
+            vmem((far, near, rows, rank), I16),
+            vmem((far, rows, rank), I16),
+            vmem((far, near, 1, rank), F32),
+            vmem((far, 1, rank), F32),
+            vmem((far, near, 1, rank), F32),
+            vmem((far, 1, rank), F32),
             vmem((tiles, width, rank), F32),
-            vmem((cells, tiles, width, rank), F32),
+            vmem((tiles, width, rank), I16),
+            vmem((tiles, 1, rank), F32),
+            vmem((cells, tiles, width, rank), I16),
+            vmem((cells, tiles, 1, rank), F32),
             vmem((1, rank), F32),
             vmem((cells, 1, rank), F32),
         ] + gather_sems(far, near) * 2 + [dma((far, near))] * 4 + [dma((far,))] * 2
-        + [dma((group,))] * 4 + [dma((cells, tiles))] * 2 + [dma((cells,))] * 2 + [dma((1,))],
+        + [dma((group,))] * 4 + [dma((cells, tiles))] * 2 + [dma((cells,))] * 2 + [dma((1,))]
+        + [dma((far, near))] * 2 + [dma((far,))] * 2 + [dma((cells, tiles))] * 2,
         compiler_params=pltpu.CompilerParams(
             collective_id=0, has_side_effects=True, vmem_limit_bytes=60 * 1024 * 1024
         ),

time: 78 us -> 76.4 us (0.979)
  Pallas kernels: 71.8 us -> 70.2 us
    pallas_call x1, Pallas kernels: 71.8 us -> 70.2 us  [step(): pl.pallas_call(functools.partial(step_kernel, group, cells), out_shape=(j...]
where the time goes in v2:
time: 76.4 us; the launch traced here: 76.2 us
  Pallas kernels  70.2 us (92%)
  local copies, waits for them, and re-layouts  3.44 us (5%)
  between operations  1.29 us (2%)
  other arithmetic  1.28 us (2%)
    pallas_call x1, Pallas kernels, step(): pl.pallas_call(functools.partial(step_kernel, group, cells), out_shape=(j...  70.2 us
    unnamed x2, local copies, waits for them, and re-layouts  3.44 us

profile of v2, /device:TPU:0, one launch (start us, length us, event | category | flops | bytes accessed | tf_op | source)
XLA Modules:
  0.0 76.2 jit_solution(9050564454179063215)
XLA Ops:
  1.3 0.7 compare_select_fusion
  2.0 0.6 select_reduce_fusion.table
  2.6 70.2 %update_step.1 = (f32[256,128]{1,0:T(8,128)}, f32[4,256,128]{2,1,0:T(8,128)}) custom-call(bf16[48,256,256]{2,1,0:T(8,128)(2,1)} %blocks.1, s32[64]{0:T(128)} %select_reduce_fusion.table, f32[256,128]{1,0:T(8,128)} %cell.1, f32[4,256,128]{2,1,0:T(8,128)} %bitcast.5), custom_call_target="tpu_custom_call" | custom-call | tf_op jit(solution)/shard_map/update_step/pallas_call | solution.py:372
  72.8 1.6 %copy.11 = f32[256,128]{1,0:T(8,128)} copy(f32[256,128]{1,0:T(8,128)} %get-tuple-element.8) | data formatting | bytes 262144
  74.3 1.9 %copy.12 = f32[1024,128]{1,0:T(8,128)} copy(f32[1024,128]{1,0:T(8,128)} %bitcast.4) | data formatting | bytes 1048576

commit v3 on v2

--- a/solution.py
+++ b/solution.py
@@ -156,22 +156,22 @@
     held[slots] = jnp.zeros((width, width), BF)
     own_bf[...] = cell[...].astype(BF)
     cell_bf[spot.me] = cell[...].astype(BF)
+    pl.semaphore_wait(pltpu.get_barrier_semaphore(), group - 1 + cells - 1)
+
+    order = far_order(far) + [0]
+    one = Gather(spot, own_bf, cell_bf, one_sems)
+    one.start(order[:-1])
     first_sum = jnp.zeros((1, gene.shape[-1]), F32)
     for j in range(tiles):
         first_sum += jnp.sum(gene[j], axis=0, keepdims=True)
     own_sum[...] = first_sum
     parts[spot.me] = first_sum
-    pl.semaphore_wait(pltpu.get_barrier_semaphore(), group - 1 + cells - 1)
-
-    order = far_order(far) + [0]
-    one = Gather(spot, own_bf, cell_bf, one_sems)
-    one.start(order[:-1])
     shared = share(spot, own_sum, parts, gs, gr)
     for j in range(tiles):
         gene_bf[j] = gene[j].astype(BF)
         flipped[j] = gene[j].astype(BF).T
+    one.take_near(0)
     load.wait()
-    one.take_near(0)
 
     def ratio_of(source, g, j):
         rows_bf = source[g]
@@ -279,32 +279,46 @@
     shared = share(spot, next_sum, next_parts, ns, nr)
     acc[...] = jnp.zeros_like(acc)
 
-    def second_half(d, core, columns):
+    def second_terms(chunks, j):
+        total = None
+        for g in chunks:
+            ratio, rows_bf = ratio_of(next_cell, g, j)
+            term = lax.dot_general(
+                ratio, rows_bf, (((0,), (0,)), ((), ())), preferred_element_type=F32
+            )
+            total = term if total is None else total + term
+        acc[j] += total
+
+    def second_chunks(d, core, first, last):
         def body(e, carry):
-            g = spot.index(spot.a_at(d), spot.b_at(e), core)
-            for j in columns:
-                ratio, rows_bf = ratio_of(next_cell, g, j)
-                acc[j] += lax.dot_general(
-                    ratio, rows_bf, (((0,), (0,)), ((), ())), preferred_element_type=F32
-                )
+            for j in every:
+                second_terms([spot.index(spot.a_at(d), spot.b_at(e), core)], j)
             return carry
 
+        lax.fori_loop(first, last, body, 0)
+
+    def second_column(offsets, j):
+        def body(e, carry):
+            second_terms([spot.index(spot.a_at(d), spot.b_at(e), core)
+                          for d in offsets for core in (0, 1)], j)
+            return carry
+
         lax.fori_loop(0, near, body, 0)
 
     every = range(tiles)
+    second_chunks(0, c, 0, 1)
     two.take_near(0)
-    two.take_far(later[0])
+    second_chunks(0, c, 1, near)
     two.ready(0)
-    second_half(0, c, every)
-    two.take_far(later[1])
-    second_half(0, 1 - c, every)
-    two.take_far(later[2])
+    second_chunks(0, 1 - c, 0, near)
+    for d in later:
+        two.take_far(d)
     two.take_near(later[0])
     two.take_near(later[1])
-    second_half(later[0], c, every)
+    two.ready(later[0])
+    second_chunks(later[0], c, 0, near)
     two.take_near(later[2])
-    two.ready(later[0])
-    second_half(later[0], 1 - c, every)
+    second_chunks(later[0], 1 - c, 0, near)
     two.ready(later[1])
     two.ready(later[2])
 
@@ -323,9 +337,7 @@
         return jnp.mean(gene_bf[j].astype(F32), axis=1, keepdims=True)
 
     for j in every:
-        for d in later[1:]:
-            for core in (0, 1):
-                second_half(d, core, [j])
+        second_column(later[1:], j)
         encode(acc[j] * balance(j), code.at[j], codem.at[j])
         other[mine, j] = code[j]
         otherm[mine, j] = codem[j]

time: 76.4 us -> 69.7 us (0.912)
  Pallas kernels: 70.2 us -> 63.5 us
    pallas_call x1, Pallas kernels: 70.2 us -> 63.5 us  [step(): pl.pallas_call(functools.partial(step_kernel, group, cells), out_shape=(j...]
where the time goes in v3:
time: 69.7 us; the launch traced here: 69.5 us
  Pallas kernels  63.5 us (91%)
  local copies, waits for them, and re-layouts  3.44 us (5%)
  between operations  1.29 us (2%)
  other arithmetic  1.28 us (2%)
    pallas_call x1, Pallas kernels, step(): pl.pallas_call(functools.partial(step_kernel, group, cells), out_shape=(j...  63.5 us
    unnamed x2, local copies, waits for them, and re-layouts  3.44 us

profile of v3, /device:TPU:0, one launch (start us, length us, event | category | flops | bytes accessed | tf_op | source)
XLA Modules:
  0.0 69.5 jit_solution(5355092207402301393)
XLA Ops:
  1.3 0.7 compare_select_fusion
  2.0 0.6 select_reduce_fusion.table
  2.6 63.5 %update_step.1 = (f32[256,128]{1,0:T(8,128)}, f32[4,256,128]{2,1,0:T(8,128)}) custom-call(bf16[48,256,256]{2,1,0:T(8,128)(2,1)} %blocks.1, s32[64]{0:T(128)} %select_reduce_fusion.table, f32[256,128]{1,0:T(8,128)} %cell.1, f32[4,256,128]{2,1,0:T(8,128)} %bitcast.5), custom_call_target="tpu_custom_call" | custom-call | tf_op jit(solution)/shard_map/update_step/pallas_call | solution.py:384
  66.0 1.6 %copy.11 = f32[256,128]{1,0:T(8,128)} copy(f32[256,128]{1,0:T(8,128)} %get-tuple-element.8) | data formatting | bytes 262144
  67.6 1.9 %copy.12 = f32[1024,128]{1,0:T(8,128)} copy(f32[1024,128]{1,0:T(8,128)} %bitcast.4) | data formatting | bytes 1048576
